TPU v7x, 32 devices: a whole 2x2x4 slice. The times are simulated.
32 devices in a mesh: freq: 8 (over z, x), pair: 4 (over y, core).
Axes of the slice: x: 2, y: 2, z: 4, core: 2. Of those that a mesh axis runs over, the one named last changes fastest.
Arguments:
- samples: bfloat16 [2048, 8, 2, 1024], P(('freq', 'pair')), may hold values from -6 to 6
- rfi_flags: int32 [8, 1024], P('freq'), may hold values 0 or 1
- feed_map: int32 [2048], replicated, may hold values from 0 to 2047, each once
Outputs:
- visibilities: bfloat16 [8, 2, 2048, 2048], P('freq', None, 'pair')
Inputs may be any that keep to these rules, and one draw needn't show every extreme that they name: `feed_map`: each of the 2048 feeds is assigned to exactly one slot.
All inputs are finite; a program needn't handle non-finite values. No bound on the sum of `rfi_flags` on one device may be relied on, other than what follows from the above.
Results may differ from a plain program's by a relative error of at most 0.001.
Values may be sent and summed in bfloat16 or wider, within the bound.
No kernel may reach another device: no remote copies, remote signals or barrier semaphores. Data moves between devices by JAX's collectives and lax.ppermute only.
A program may use at most 64 MiB of HBM per device.

v0:
```python
import jax
import jax.numpy as jnp
from jax import lax
from jax.sharding import PartitionSpec as P


def local(samples, rfi_flags, feed_map):
    n_pair = lax.axis_size("pair")
    n_freq = lax.axis_size("freq")
    member = lax.axis_index("pair")
    keep_mask = (1 - rfi_flags).astype(jnp.bfloat16)
    shard_feeds = samples.shape[0]
    turned = lax.all_to_all(samples, "freq", split_axis=1, concat_axis=0, tiled=True)
    turned = turned * keep_mask[None, :, None, :]
    kept = lax.all_gather(turned, "pair", axis=0, tiled=True)
    shard_index = feed_map // shard_feeds
    within = feed_map % shard_feeds
    position = (
        shard_index % n_pair * (n_freq * shard_feeds) + shard_index // n_pair * shard_feeds + within
    )
    feed_count = kept.shape[0]
    steps_time = kept.shape[3]
    row_count = feed_count // n_pair
    inverse = 1.0 / steps_time
    feeds_all = kept[:, 0].reshape(feed_count, 2 * steps_time)
    columns = jnp.take(feeds_all, position, axis=0)
    own_rows = lax.dynamic_slice_in_dim(columns, member * row_count, row_count, 0)
    rotated_rows = jnp.concatenate([own_rows[:, steps_time:], -own_rows[:, :steps_time]], axis=1)
    stacked = jnp.concatenate([own_rows, rotated_rows], axis=0)
    product = lax.dot_general(
        stacked, columns, (((1,), (1,)), ((), ())), preferred_element_type=jnp.float32
    )
    results = [(product * inverse).astype(jnp.bfloat16).reshape(2, row_count, columns.shape[0])]
    computed = jnp.stack(results, axis=0)
    return computed


def solution(mesh):
    in_specs = (P(("freq", "pair"), None, None, None), P("freq", None), P())
    out_specs = P("freq", None, "pair", None)
    return jax.shard_map(local, mesh=mesh, in_specs=in_specs, out_specs=out_specs, check_vma=False)
```

profile of v0, /device:TPU:0, one launch (start us, length us, event | category | flops | bytes accessed | tf_op | source)
XLA Modules:
  0.0 202.3 jit_solution(14040332480941497455)
XLA Ops:
  6.5 0.0 copy-start.2
  6.5 4.1 %copy.6 = bf16[64,8,2,1024]{3,0,2,1:T(8,128)(2,1)} copy(bf16[64,8,2,1024]{3,2,1,0:T(2,128)(2,1)} %param.3) | data formatting | bytes 4194304 | tf_op args[0]
  10.6 0.0 copy-start.1
  10.6 7.4 %all-to-all-start = ((bf16[64,8,2,1024]{3,0,2,1:T(8,128)(2,1)}), bf16[64,8,2,1024]{3,0,2,1:T(8,128)(2,1)S(1)}, u32[]{:S(2)}, u32[]{:S(2)}) async-start(bf16[64,8,2,1024]{3,0,2,1:T(8,128)(2,1)} %copy.6), calls=%async_computation | async-start | bytes 4194304 | tf_op jit(solution)/shard_map/all_to_all | solution.py:13
  18.0 0.0 all-gather.2.cloned.1.call-start
  18.1 0.0 copy-done.2
  18.1 48.2 %all-to-all-done = bf16[64,8,2,1024]{3,0,2,1:T(8,128)(2,1)S(1)} async-done(((bf16[64,8,2,1024]{3,0,2,1:T(8,128)(2,1)}), bf16[64,8,2,1024]{3,0,2,1:T(8,128)(2,1)S(1)}, u32[]{:S(2)}, u32[]{:S(2)}) %all-to-all-start) | async-done | bytes 2097184 | tf_op jit(solution)/shard_map/all_to_all | solution.py:13
  66.3 0.2 copy.7
  66.4 1.6 bitcast_multiply_fusion
  68.0 0.0 all-gather.2.cloned.1.call-update
  68.1 0.0 copy-done.1
  68.1 57.4 %all-gather.2.cloned.1.call-done = bf16[2048,1,2,1024]{3,0,2,1:T(8,128)(2,1)} async-done(((bf16[512,1,2,1024]{3,0,2,1:T(8,128)(2,1)}), bf16[2048,1,2,1024]{3,0,2,1:T(8,128)(2,1)}) %all-gather.2.cloned.1.call-update) | async-done | bytes 8388624 | tf_op jit(solution)/shard_map/all_gather | solution.py:15
  125.6 16.4 %copy.8 = bf16[2048,1,2,1024]{3,2,0,1:T(2,128)(2,1)} copy(bf16[2048,1,2,1024]{3,0,2,1:T(8,128)(2,1)} %all-gather.2.cloned.1.call-done) | data formatting | bytes 16777216 | tf_op jit(solution)/shard_map/all_gather | solution.py:15
  142.0 10.1 %copy.9 = bf16[256,8,2,1024]{3,1,2,0:T(8,128)(2,1)} copy(bf16[256,8,2,1024]{3,2,1,0:T(2,128)(2,1)} %bitcast.13) | data formatting | bytes 16777216
  152.1 20.8 %gather_fusion = bf16[2048,2048]{1,0:T(8,128)(2,1)} fusion(bf16[2048,2048]{1,0:T(8,128)(2,1)} %bitcast.12, s32[2048]{0:T(1024)S(1)} %broadcast_clamp_fusion), kind=kCustom, calls=%fused_computation | custom fusion | bytes 16785408 | tf_op jit(solution)/shard_map/jit(_take)/gather | solution.py:26
  172.9 7.5 %broadcast_select_fusion = bf16[2048,2048]{1,0:T(8,128)(2,1)} fusion(bf16[2048,2048]{1,0:T(8,128)(2,1)} %gather_fusion, pred[2048]{0:T(1024)(128)(4,1)S(1)} %get-tuple-element.5), kind=kLoop, calls=%fused_computation.2 | loop fusion | flops 4194304 | bytes 16779264 | tf_op jit(solution)/shard_map/jit(_take)/select_n | solution.py:26
  180.4 0.0 copy-start
  180.4 1.9 constant_dynamic-slice_fusion
  182.3 2.2 %fusion.16 = (bf16[512,1024]{1,0:T(8,128)(2,1)S(1)}, bf16[512,1024]{1,0:T(8,128)(2,1)S(1)}) fusion(bf16[2048,2048]{1,0:T(8,128)(2,1)} %broadcast_select_fusion, s32[]{:T(128)S(6)} %select_n.36, s32[]{:T(128)S(6)} %add.37), kind=kLoop, calls=%fused_computation.38 | loop fusion | flops 1572864 | bytes 4194312 | tf_op jit(solution)/shard_map/slice | solution.py:28
  184.4 0.6 copy-done
  185.0 10.4 %multiply_convert_fusion = bf16[1024,2048]{1,0:T(8,128)(2,1)} fusion(bf16[2048,2048]{1,0:T(8,128)(2,1)S(1)} %copy-done, bf16[512,1024]{1,0:T(8,128)(2,1)S(1)} %get-tuple-element.8, bf16[512,1024]{1,0:T(8,128)(2,1)S(1)} %get-tuple-element.7, bf16[512,2048]{1,0:T(8,128)(2,1)S(1)} %constant_dynamic-slice_fusion), kind=kOutput, calls=%fused_computation.1 | convolution fusion | flops 8606711808 | bytes 16777216 | tf_op jit(solution)/shard_map/dot_general | solution.py:30
  (3 shorter events, 0.1 us)
Async XLA Ops:
  6.5 11.5 %copy-start.2 = (s32[1,1024]{1,0:T(1,128)S(1)}, s32[1,1024]{1,0:T(1,128)}, u32[]{:S(2)}) copy-start(s32[1,1024]{1,0:T(1,128)} %param.4) | copy-start | bytes 12292
  10.6 57.5 %copy-start.1 = (s32[2048]{0:T(1024)S(1)}, s32[2048]{0:T(1024)}, u32[]{:S(2)}) copy-start(s32[2048]{0:T(1024)} %param.5) | copy-start | bytes 24580
  10.6 55.7 %all-to-all-start = ((bf16[64,8,2,1024]{3,0,2,1:T(8,128)(2,1)}), bf16[64,8,2,1024]{3,0,2,1:T(8,128)(2,1)S(1)}, u32[]{:S(2)}, u32[]{:S(2)}) async-start(bf16[64,8,2,1024]{3,0,2,1:T(8,128)(2,1)} %copy.6), calls=%async_computation | async-start | bytes 4194304 | tf_op jit(solution)/shard_map/all_to_all | solution.py:13
  18.0 107.5 %all-gather.2.cloned.1.call-start = ((), (), s32[]{:S(2)}) async-start(), calls=%async_computation.1 | async-start | bytes 10485760 | tf_op jit(solution)/shard_map/all_gather | solution.py:15
  180.4 4.6 %copy-start = (bf16[2048,2048]{1,0:T(8,128)(2,1)S(1)}, bf16[2048,2048]{1,0:T(8,128)(2,1)}, u32[]{:S(2)}) copy-start(bf16[2048,2048]{1,0:T(8,128)(2,1)} %broadcast_select_fusion) | copy-start | bytes 25165828
Sparse Core Ops, SparseCore 0:
  68.2 57.3 all-gather.1
where the time goes:
time: 203 us; the launch traced here: 202 us
  waiting for transfers between devices  106 us (52%)
  local copies, waits for them, and re-layouts  54.1 us (27%)
  between operations  13.5 us (7%)
  other arithmetic  11.3 us (6%)
  matrix products  10.4 us (5%)
  starting transfers between devices  7.45 us (4%)
    all_gather x1, waiting for transfers between devices, local(): kept = lax.all_gather(turned, 'pair', axis=0, tiled=True)  57.4 us
    all_to_all x1, waiting for transfers between devices, local(): lax.all_to_all(samples, 'freq', split_axis=1, concat_axis=0, tiled=True)  48.2 us
    gather x1, local copies, waits for them, and re-layouts, local(): columns = jnp.take(feeds_all, position, axis=0)  20.8 us
    all_gather x1, local copies, waits for them, and re-layouts, local(): kept = lax.all_gather(turned, 'pair', axis=0, tiled=True)  16.4 us
    unnamed x8, local copies, waits for them, and re-layouts  14.8 us
    dot_general x1, matrix products, local(): lax.dot_general(stacked, columns, (((1,), (1,)), ((), ())), preferred_ele...  10.4 us
    select_n x1, other arithmetic, local(): columns = jnp.take(feeds_all, position, axis=0)  7.45 us
    all_to_all x1, starting transfers between devices, local(): lax.all_to_all(samples, 'freq', split_axis=1, concat_axis=0, tiled=True)  7.41 us
  transfers between devices with their start and end apart: 2, of which 2 were waited for; matrix products, arithmetic and copies ran while one was open for 0% of the time, Pallas kernels for 0%

commit v1 on v0

--- a/solution.py
+++ b/solution.py
@@ -2,6 +2,22 @@
 import jax.numpy as jnp
 from jax import lax
 from jax.sharding import PartitionSpec as P
+
+
+def swapped_with_each(x, axis, split, join):
+    ways, here = (lax.axis_size(axis), lax.axis_index(axis))
+    width = x.shape[split] // ways
+    shape = list(x.shape)
+    shape[split] = width
+    height = shape[join]
+    shape[join] = height * ways
+    full = jnp.zeros(shape, x.dtype)
+    for mask in range(ways):
+        part = lax.dynamic_slice_in_dim(x, (here ^ mask) * width, width, axis=split)
+        if mask:
+            part = lax.ppermute(part, axis, [(d, d ^ mask) for d in range(ways)])
+        full = lax.dynamic_update_slice_in_dim(full, part, (here ^ mask) * height, axis=join)
+    return full
 
 
 def local(samples, rfi_flags, feed_map):
@@ -10,7 +26,7 @@
     member = lax.axis_index("pair")
     keep_mask = (1 - rfi_flags).astype(jnp.bfloat16)
     shard_feeds = samples.shape[0]
-    turned = lax.all_to_all(samples, "freq", split_axis=1, concat_axis=0, tiled=True)
+    turned = swapped_with_each(samples, "freq", 1, 0)
     turned = turned * keep_mask[None, :, None, :]
     kept = lax.all_gather(turned, "pair", axis=0, tiled=True)
     shard_index = feed_map // shard_feeds

time: 203 us -> 187 us (0.921)
  waiting for transfers between devices: 106 us -> 90.6 us
  local copies, waits for them, and re-layouts: 54.1 us -> 44.9 us
  starting transfers between devices: 7.45 us -> 13.8 us
    all_to_all x1 -> x0, waiting for transfers between devices: 48.2 us -> none  [local(): lax.all_to_all(samples, 'freq', split_axis=1, concat_axis=0, tiled=True)]
    ppermute x0 -> x7, waiting for transfers between devices: none -> 25.7 us  [swapped_with_each(): part = lax.ppermute(part, axis, [(d, d ^ mask) for d in range(ways)])]
    all_gather x1 -> x0, local copies, waits for them, and re-layouts: 16.4 us -> none  [local(): kept = lax.all_gather(turned, 'pair', axis=0, tiled=True)]
    ppermute x0 -> x7, starting transfers between devices: none -> 13.8 us  [swapped_with_each(): part = lax.ppermute(part, axis, [(d, d ^ mask) for d in range(ways)])]
    all_gather x1, waiting for transfers between devices: 57.4 us -> 64.9 us  [local(): kept = lax.all_gather(turned, 'pair', axis=0, tiled=True)]
    all_to_all x1 -> x0, starting transfers between devices: 7.41 us -> none  [local(): lax.all_to_all(samples, 'freq', split_axis=1, concat_axis=0, tiled=True)]
    dynamic_update_slice x0 -> x7, local copies, waits for them, and re-layouts: none -> 6.19 us  [swapped_with_each(): lax.dynamic_update_slice_in_dim(full, part, (here ^ mask) * height, axis=...]
    dynamic_slice x0 -> x1, local copies, waits for them, and re-layouts: none -> 2.92 us  [swapped_with_each(): part = lax.dynamic_slice_in_dim(x, (here ^ mask) * width, width, axis=split)]
  transfers between devices with their start and end apart: 2 -> 8, of which waited for: 2 -> 5; matrix products, arithmetic and copies ran while one was open for 0% -> 3% of each run, Pallas kernels for 0% -> 0%
where the time goes in v1:
time: 187 us; the launch traced here: 186 us
  waiting for transfers between devices  90.6 us (48%)
  local copies, waits for them, and re-layouts  44.9 us (24%)
  starting transfers between devices  13.8 us (7%)
  between operations  13.5 us (7%)
  other arithmetic  12.8 us (7%)
  matrix products  10.4 us (6%)
    all_gather x1, waiting for transfers between devices, local(): kept = lax.all_gather(turned, 'pair', axis=0, tiled=True)  64.9 us
    ppermute x7, waiting for transfers between devices, swapped_with_each(): part = lax.ppermute(part, axis, [(d, d ^ mask) for d in range(ways)])  25.7 us
    gather x1, local copies, waits for them, and re-layouts, local(): columns = jnp.take(feeds_all, position, axis=0)  21 us
    ppermute x7, starting transfers between devices, swapped_with_each(): part = lax.ppermute(part, axis, [(d, d ^ mask) for d in range(ways)])  13.8 us
    unnamed x9, local copies, waits for them, and re-layouts  11.9 us
    dot_general x1, matrix products, local(): lax.dot_general(stacked, columns, (((1,), (1,)), ((), ())), preferred_ele...  10.4 us
    select_n x1, other arithmetic, local(): columns = jnp.take(feeds_all, position, axis=0)  7.45 us
    dynamic_update_slice x7, local copies, waits for them, and re-layouts, swapped_with_each(): lax.dynamic_update_slice_in_dim(full, part, (here ^ mask) * height, axis=...  6.19 us
  transfers between devices with their start and end apart: 8, of which 5 were waited for; matrix products, arithmetic and copies ran while one was open for 3% of the time, Pallas kernels for 0%

profile of v1, /device:TPU:0, one launch (start us, length us, event | category | flops | bytes accessed | tf_op | source)
XLA Modules:
  0.0 186.1 jit_solution(1252524181165227011)
XLA Ops:
  6.5 1.1 broadcast_in_dim.17
  7.6 0.5 copy-done.1
  8.1 2.9 %constant_dynamic-slice_fusion.1 = (bf16[64,1,2,1024]{3,2,1,0:T(2,128)(2,1)S(1)}, bf16[64,1,2,1024]{3,2,1,0:T(2,128)(2,1)S(1)}, bf16[64,1,2,1024]{3,2,1,0:T(2,12...) fusion(bf16[64,8,2,1024]{3,2,1,0:T(2,128)(2,1)S(1)} %copy-done., ...), kind=kLoop, calls=%fused_computation.37 | loop fusion | bytes 4194340 | tf_op jit(solution)/shard_map/dynamic_slice | solution.py:16
  11.1 3.0 %collective-permute-start = (bf16[64,1,2,1024]{3,2,1,0:T(2,128)(2,1)}, bf16[64,1,2,1024]{3,2,1,0:T(2,128)(2,1)}, u32[]{:S(2)}, u32[]{:S(2)}) collective-permute-start(bf16[64,1,2,1024]{3,2,1,0:T(2,128)(2,1)} %get-tuple-element.14), channel_id=1, source_target_pairs={{0,4},{4,0},{8,12},{12,8},{16,20},{20,16},{24,28},{28,24},{1,5},{5... | collective-permute-start | bytes 786440 | tf_op jit(solution)/shard_map/ppermute | solution.py:18
  14.0 1.6 collective-permute-start.1
  15.6 3.0 %collective-permute-start.3 = (bf16[64,1,2,1024]{3,2,1,0:T(2,128)(2,1)S(1)}, bf16[64,1,2,1024]{3,2,1,0:T(2,128)(2,1)}, u32[]{:S(2)}, u32[]{:S(2)}) collective-permute-start(bf16[64,1,2,1024]{3,2,1,0:T(2,128)(2,1)S(1)} %get-tuple-element.11), channel_id=1, source_target_pairs={{0,16},{4,20},{8,24},{12,28},{16,0},{20,4},{24,8},{28,12},{1,17},{... | collective-permute-start | bytes 786440 | tf_op jit(solution)/shard_map/ppermute | solution.py:18
  18.6 1.3 collective-permute-start.4
  20.0 0.7 collective-permute-done
  20.6 3.8 %collective-permute-start.5 = (bf16[64,1,2,1024]{3,2,1,0:T(2,128)(2,1)S(1)}, bf16[64,1,2,1024]{3,2,1,0:T(2,128)(2,1)S(1)}, u32[]{:S(2)}, u32[]{:S(2)}) collective-permute-start(bf16[64,1,2,1024]{3,2,1,0:T(2,128)(2,1)S(1)} %get-tuple-element.16), channel_id=1, source_target_pairs={{0,24},{4,28},{8,16},{12,20},{16,8},{20,12},{24,0},{28,4},{1,25},{... | collective-permute-start | bytes 786440 | tf_op jit(solution)/shard_map/ppermute | solution.py:18
  24.5 1.2 constant_dynamic-update-slice_fusion.6
  25.6 8.3 %collective-permute-done.1 = bf16[64,1,2,1024]{3,2,1,0:T(2,128)(2,1)} collective-permute-done((bf16[64,1,2,1024]{3,2,1,0:T(2,128)(2,1)}, bf16[64,1,2,1024]{3,2,1,0:T(2,128)(2,1)}, u32[]{:S(2)}, u32[]{:S(2)}) %collective-permute-start.1) | collective-permute-done | bytes 262176 | tf_op jit(solution)/shard_map/ppermute | solution.py:18
  33.9 1.1 collective-permute-start.6
  35.1 1.2 constant_dynamic-update-slice_fusion.5
  36.2 1.1 collective-permute-done.2
  37.3 1.2 constant_dynamic-update-slice_fusion.4
  38.5 1.2 constant_dynamic-update-slice_fusion.3
  39.6 15.6 %collective-permute-done.4 = bf16[64,1,2,1024]{3,2,1,0:T(2,128)(2,1)} collective-permute-done((bf16[64,1,2,1024]{3,2,1,0:T(2,128)(2,1)S(1)}, bf16[64,1,2,1024]{3,2,1,0:T(2,128)(2,1)}, u32[]{:S(2)}, u32[]{:S(2)}) %collective-permute-start.4) | collective-permute-done | bytes 262176 | tf_op jit(solution)/shard_map/ppermute | solution.py:18
  55.2 1.2 constant_dynamic-update-slice_fusion.2
  56.4 0.0 collective-permute-done.5
  56.4 0.2 constant_dynamic-update-slice_fusion.1
  56.6 0.2 constant_dynamic-update-slice_fusion
  56.8 3.1 %broadcast_multiply_fusion = bf16[512,1,2,1024]{3,2,1,0:T(2,128)(2,1)} fusion(bf16[512,1,2,1024]{3,2,1,0:T(2,128)(2,1)S(1)} %constant_dynamic-update-slice_fusion, bf16[1024]{0:T(1024)(128)(2,1)S(1)} %convert_reduce_fusion), kind=kLoop, calls=%fused_computation.9 | loop fusion | flops 1048576 | bytes 4196352 | tf_op jit(solution)/shard_map/mul | solution.py:30
  59.9 0.0 all-gather.2.cloned.1.call-update
  60.0 0.7 copy-done.2
  60.7 64.9 %all-gather.2.cloned.1.call-done = bf16[2048,1,2,1024]{3,2,1,0:T(2,128)(2,1)} async-done(((bf16[512,1,2,1024]{3,2,1,0:T(2,128)(2,1)}), bf16[2048,1,2,1024]{3,2,1,0:T(2,128)(2,1)}) %all-gather.2.cloned.1.call-update) | async-done | bytes 8388624 | tf_op jit(solution)/shard_map/all_gather | solution.py:31
  125.6 10.1 %copy.12 = bf16[256,8,2,1024]{3,1,2,0:T(8,128)(2,1)} copy(bf16[256,8,2,1024]{3,2,1,0:T(2,128)(2,1)} %bitcast.6) | data formatting | bytes 16777216
  135.7 21.0 %gather_fusion = bf16[2048,2048]{1,0:T(8,128)(2,1)} fusion(bf16[2048,2048]{1,0:T(8,128)(2,1)} %bitcast.5, s32[2048]{0:T(1024)S(1)} %broadcast_clamp_fusion), kind=kCustom, calls=%fused_computation | custom fusion | bytes 16785408 | tf_op jit(solution)/shard_map/jit(_take)/gather | solution.py:42
  156.7 7.5 %broadcast_select_fusion = bf16[2048,2048]{1,0:T(8,128)(2,1)} fusion(bf16[2048,2048]{1,0:T(8,128)(2,1)} %gather_fusion, pred[2048]{0:T(1024)(128)(4,1)S(1)} %get-tuple-element.5), kind=kLoop, calls=%fused_computation.2 | loop fusion | flops 4194304 | bytes 16779264 | tf_op jit(solution)/shard_map/jit(_take)/select_n | solution.py:42
  164.2 1.9 %constant_dynamic-slice_fusion = bf16[512,2048]{1,0:T(8,128)(2,1)S(1)} fusion(bf16[2048,2048]{1,0:T(8,128)(2,1)} %broadcast_select_fusion, s32[]{:T(128)S(6)} %select_n.100), kind=kLoop, calls=%fused_computation.35 | loop fusion | bytes 4194308 | tf_op jit(solution)/shard_map/dynamic_slice | solution.py:43
  166.0 2.2 %fusion.16 = (bf16[512,1024]{1,0:T(8,128)(2,1)S(1)}, bf16[512,1024]{1,0:T(8,128)(2,1)S(1)}) fusion(bf16[2048,2048]{1,0:T(8,128)(2,1)} %broadcast_select_fusion, s32[]{:T(128)S(6)} %select_n.100, s32[]{:T(128)S(6)} %add.101), kind=kLoop, calls=%fused_computation.53 | loop fusion | flops 1572864 | bytes 4194312 | tf_op jit(solution)/shard_map/slice | solution.py:44
  168.2 0.6 copy-done
  168.8 10.4 %multiply_convert_fusion = bf16[1024,2048]{1,0:T(8,128)(2,1)} fusion(bf16[2048,2048]{1,0:T(8,128)(2,1)S(1)} %copy-done, bf16[512,1024]{1,0:T(8,128)(2,1)S(1)} %get-tuple-element.8, bf16[512,1024]{1,0:T(8,128)(2,1)S(1)} %get-tuple-element.7, bf16[512,2048]{1,0:T(8,128)(2,1)S(1)} %constant_dynamic-slice_fusion), kind=kOutput, calls=%fused_computation.1 | convolution fusion | flops 8606711808 | bytes 16777216 | tf_op jit(solution)/shard_map/dot_general | solution.py:46
  (12 shorter events, 0.1 us)
Async XLA Ops:
  6.5 119.1 %all-gather.2.cloned.1.call-start = ((), (), s32[]{:S(2)}) async-start(), calls=%async_computation | async-start | bytes 10485760 | tf_op jit(solution)/shard_map/all_gather | solution.py:31
  6.5 1.6 copy-start.1
  8.1 11.7 %copy-start.3 = (s32[1,1024]{1,0:T(1,128)S(1)}, s32[1,1024]{1,0:T(1,128)}, u32[]{:S(2)}) copy-start(s32[1,1024]{1,0:T(1,128)} %param.4) | copy-start | bytes 12292
  11.1 9.6 %collective-permute-start = (bf16[64,1,2,1024]{3,2,1,0:T(2,128)(2,1)}, bf16[64,1,2,1024]{3,2,1,0:T(2,128)(2,1)}, u32[]{:S(2)}, u32[]{:S(2)}) collective-permute-start(bf16[64,1,2,1024]{3,2,1,0:T(2,128)(2,1)} %get-tuple-element.14), channel_id=1, source_target_pairs={{0,4},{4,0},{8,12},{12,8},{16,20},{20,16},{24,28},{28,24},{1,5},{5... | collective-permute-start | bytes 786440 | tf_op jit(solution)/shard_map/ppermute | solution.py:18
  14.0 19.9 %collective-permute-start.1 = (bf16[64,1,2,1024]{3,2,1,0:T(2,128)(2,1)}, bf16[64,1,2,1024]{3,2,1,0:T(2,128)(2,1)}, u32[]{:S(2)}, u32[]{:S(2)}) collective-permute-start(bf16[64,1,2,1024]{3,2,1,0:T(2,128)(2,1)} %get-tuple-element.13), channel_id=1, source_target_pairs={{0,8},{4,12},{8,0},{12,4},{16,24},{20,28},{24,16},{28,20},{1,9},{5... | collective-permute-start | bytes 786440 | tf_op jit(solution)/shard_map/ppermute | solution.py:18
  15.6 21.7 %collective-permute-start.2 = (bf16[64,1,2,1024]{3,2,1,0:T(2,128)(2,1)S(1)}, bf16[64,1,2,1024]{3,2,1,0:T(2,128)(2,1)}, u32[]{:S(2)}, u32[]{:S(2)}) collective-permute-start(bf16[64,1,2,1024]{3,2,1,0:T(2,128)(2,1)S(1)} %get-tuple-element.12), channel_id=1, source_target_pairs={{0,12},{4,8},{8,4},{12,0},{16,28},{20,24},{24,20},{28,16},{1,13},{... | collective-permute-start | bytes 786440 | tf_op jit(solution)/shard_map/ppermute | solution.py:18
  15.6 22.8 %collective-permute-start.3 = (bf16[64,1,2,1024]{3,2,1,0:T(2,128)(2,1)S(1)}, bf16[64,1,2,1024]{3,2,1,0:T(2,128)(2,1)}, u32[]{:S(2)}, u32[]{:S(2)}) collective-permute-start(bf16[64,1,2,1024]{3,2,1,0:T(2,128)(2,1)S(1)} %get-tuple-element.11), channel_id=1, source_target_pairs={{0,16},{4,20},{8,24},{12,28},{16,0},{20,4},{24,8},{28,12},{1,17},{... | collective-permute-start | bytes 786440 | tf_op jit(solution)/shard_map/ppermute | solution.py:18
  18.6 36.6 %collective-permute-start.4 = (bf16[64,1,2,1024]{3,2,1,0:T(2,128)(2,1)S(1)}, bf16[64,1,2,1024]{3,2,1,0:T(2,128)(2,1)}, u32[]{:S(2)}, u32[]{:S(2)}) collective-permute-start(bf16[64,1,2,1024]{3,2,1,0:T(2,128)(2,1)S(1)} %get-tuple-element.10), channel_id=1, source_target_pairs={{0,20},{4,16},{8,28},{12,24},{16,4},{20,0},{24,12},{28,8},{1,21},{... | collective-permute-start | bytes 786440 | tf_op jit(solution)/shard_map/ppermute | solution.py:18
  20.6 35.7 %collective-permute-start.5 = (bf16[64,1,2,1024]{3,2,1,0:T(2,128)(2,1)S(1)}, bf16[64,1,2,1024]{3,2,1,0:T(2,128)(2,1)S(1)}, u32[]{:S(2)}, u32[]{:S(2)}) collective-permute-start(bf16[64,1,2,1024]{3,2,1,0:T(2,128)(2,1)S(1)} %get-tuple-element.16), channel_id=1, source_target_pairs={{0,24},{4,28},{8,16},{12,20},{16,8},{20,12},{24,0},{28,4},{1,25},{... | collective-permute-start | bytes 786440 | tf_op jit(solution)/shard_map/ppermute | solution.py:18
  33.9 22.7 %collective-permute-start.6 = (bf16[64,1,2,1024]{3,2,1,0:T(2,128)(2,1)S(1)}, bf16[64,1,2,1024]{3,2,1,0:T(2,128)(2,1)S(1)}, u32[]{:S(2)}, u32[]{:S(2)}) collective-permute-start(bf16[64,1,2,1024]{3,2,1,0:T(2,128)(2,1)S(1)} %get-tuple-element.9), channel_id=1, source_target_pairs={{0,28},{4,24},{8,20},{12,16},{16,12},{20,8},{24,4},{28,0},{1,29},{... | collective-permute-start | bytes 786440 | tf_op jit(solution)/shard_map/ppermute | solution.py:18
  59.9 0.7 copy-start.2
  164.2 4.6 %copy-start = (bf16[2048,2048]{1,0:T(8,128)(2,1)S(1)}, bf16[2048,2048]{1,0:T(8,128)(2,1)}, u32[]{:S(2)}) copy-start(bf16[2048,2048]{1,0:T(8,128)(2,1)} %broadcast_select_fusion) | copy-start | bytes 25165828
Sparse Core Ops, SparseCore 0:
  60.1 65.4 all-gather.1
